TPU v7x, 32 devices: a whole 2x2x4 slice. The times are simulated.
32 devices in a mesh: grp: 2 (over y), trade: 4 (over z), date: 2 (over x), path: 2 (over core).
Axes of the slice: x: 2, y: 2, z: 4, core: 2. Of those that a mesh axis runs over, the one named last changes fastest.
Arguments:
- driver_increments: float32 [16, 256, 128], P(('grp', 'date'), 'path'), parts along dimension 0, may hold values from -4 to 4
- persistence_ratio: float32 [16, 128], P(('grp', 'date')), parts along dimension 0, may hold values from 0 to 1, as said below
- deal_sensitivity: bfloat16 [128, 65536], P(None, ('grp', 'trade')), parts along dimension 1, may hold values from -0.5 to 0.5
- signed_notional: float32 [65536], P(('grp', 'trade')), parts along dimension 0, may hold values from -0.4 to 0.4
- batch_obligor: int32 [512], P(('grp', 'trade')), parts along dimension 0, may hold values from 0 to 127, as said below
- collateral_ceiling: float32 [256], P(('grp', 'trade')), parts along dimension 0, may hold values from -1 to 1
- default_discount_mass: float32 [16, 128], P(('grp', 'date'), 'trade'), parts along dimension 0, may hold values from 0.1 to 1
Outputs:
- exposure_profile: float32 [16, 128], P(('grp', 'date'), 'trade'), parts along dimension 0
- shock_gradient: float32 [16, 256, 128], P(('grp', 'date'), 'path'), parts along dimension 0
There are 2 independent parts, one for each index of `grp`. A program takes and returns all parts, laid end to end along the dimension named above; each array names one. Nothing has to cross between parts.
Inputs may be any that keep to these rules, and one draw needn't show every extreme that they name: `persistence_ratio`: strictly between 0 and 1. `batch_obligor`: counterparty c belongs to trade shard c // 32. Of the 64 trade blocks of one trade shard, at most 32 have counterparties on any one trade shard, and in every trade shard some counterparty shard receives exactly 32 of them.
All inputs are finite; a program needn't handle non-finite values.
Results may differ from a plain program's by a relative error of at most 0.0019.
Values sent between devices are 32-bit elements; how exact they have to be, the bound alone decides.
No kernel may reach another device: no remote copies, remote signals or barrier semaphores. Data moves between devices by JAX's collectives and lax.ppermute only.
A program may use at most 64 MiB of HBM per device.

v0:
```python
import jax
import jax.numpy as jnp
from jax import lax
from jax.sharding import PartitionSpec as P

block_width = 128
cluster_extent = 512
highest = lax.Precision.HIGHEST


def entering(value, axis, combine, identity, reverse):
    length, index = (lax.axis_size(axis), lax.axis_index(axis))
    everything = jax.tree.map(lambda part: lax.all_gather(part, axis), value)
    start = jax.tree.map(
        lambda part, zero: jnp.broadcast_to(jnp.asarray(zero, part.dtype), part.shape),
        value,
        identity,
    )

    def hop(k, before):
        at = length - 1 - k if reverse else k
        reached = at > index if reverse else at < index
        new = combine(before, jax.tree.map(lambda part: part[at], everything))
        return jax.tree.map(lambda a, b: jnp.where(reached, a, b), new, before)

    return lax.fori_loop(0, length, hop, start)


def compose(earlier, later):
    return (later[0] * earlier[0], later[0] * earlier[1] + later[1])


def reverse_chain(direct, persistence_ratio):
    date_count = direct.shape[0]
    factor_gain = jnp.ones((direct.shape[2],), jnp.float32)
    message = jnp.zeros(direct.shape[1:], jnp.float32)
    for date_step in reversed(range(date_count)):
        message = persistence_ratio[date_step][None, :] * (direct[date_step] + message)
        factor_gain = persistence_ratio[date_step] * factor_gain
    identity = (jnp.ones_like(factor_gain), jnp.zeros_like(message))
    _, arriving = entering((factor_gain, message), "date", compose, identity, True)
    adjoints = []
    message = arriving
    for date_step in reversed(range(date_count)):
        adjoint = direct[date_step] + message
        adjoints.append(adjoint)
        message = persistence_ratio[date_step][None, :] * adjoint
    return jnp.stack(adjoints[::-1])


def shards(
    driver_increments,
    persistence_ratio,
    deal_sensitivity,
    signed_notional,
    batch_obligor,
    collateral_ceiling,
    default_discount_mass,
):
    date_count, path_count, factor_count = driver_increments.shape
    factor_gain = jnp.ones((factor_count,), jnp.float32)
    carried = jnp.zeros((path_count, factor_count), jnp.float32)
    for date_step in range(date_count):
        carried = persistence_ratio[date_step][None, :] * carried + driver_increments[date_step]
        factor_gain = persistence_ratio[date_step] * factor_gain
    identity = (jnp.ones_like(factor_gain), jnp.zeros_like(carried))
    _, arriving = entering((factor_gain, carried), "date", compose, identity, False)
    states = []
    carried = arriving
    for date_step in range(date_count):
        carried = persistence_ratio[date_step][None, :] * carried + driver_increments[date_step]
        states.append(carried)
    row_count = date_count * path_count
    state_bf = jnp.stack(states).reshape(row_count, factor_count).astype(jnp.bfloat16)
    deal_ordinal = deal_sensitivity.shape[1]
    block_count = deal_ordinal // block_width
    cluster_ordinal = deal_ordinal // cluster_extent
    per_group = cluster_extent // block_width

    def value_group(group_index, block_sums):
        opening_offset = group_index * cluster_extent
        sensitivity_portion = lax.dynamic_slice_in_dim(
            deal_sensitivity, opening_offset, cluster_extent, 1
        )
        size_part = lax.dynamic_slice_in_dim(signed_notional, opening_offset, cluster_extent, 0)
        linear = jnp.dot(state_bf, sensitivity_portion, preferred_element_type=jnp.float32)
        trade_value = jax.nn.softplus(linear) * size_part[None, :]
        summed = trade_value.reshape(row_count, per_group, block_width).sum(axis=2)
        return lax.dynamic_update_slice_in_dim(block_sums, summed.T, group_index * per_group, 0)

    block_sums = lax.fori_loop(
        0, cluster_ordinal, value_group, jnp.zeros((block_count, row_count), jnp.float32)
    )
    cpty_dev = collateral_ceiling.shape[0]
    shard_count = lax.axis_size("trade")
    ownership = (
        batch_obligor[:, None] == jnp.arange(cpty_dev * shard_count, dtype=jnp.int32)[None, :]
    ).astype(jnp.float32)
    partial_value = lax.dot_general(
        ownership, block_sums, (((0,), (0,)), ((), ())), precision=highest
    )
    netted = lax.psum_scatter(partial_value, "trade", scatter_dimension=0, tiled=True)
    shifted = netted - collateral_ceiling[:, None]
    exposure = jax.nn.softplus(shifted).reshape(cpty_dev, date_count, path_count)
    path_total = lax.psum(jnp.sum(exposure, axis=2).T, "path")
    exposure_profile = path_total / (path_count * lax.axis_size("path"))
    net_adjoint = (
        default_discount_mass.T[:, :, None]
        * jax.nn.sigmoid(shifted).reshape(cpty_dev, date_count, path_count)
    ).reshape(cpty_dev, row_count)
    gathered = lax.all_gather(net_adjoint, "trade", axis=0, tiled=True)
    block_adjoint = jnp.dot(ownership, gathered, precision=highest)

    def pull_group(group_index, running):
        opening_offset = group_index * cluster_extent
        sensitivity_portion = lax.dynamic_slice_in_dim(
            deal_sensitivity, opening_offset, cluster_extent, 1
        )
        size_part = lax.dynamic_slice_in_dim(signed_notional, opening_offset, cluster_extent, 0)
        linear = jnp.dot(state_bf, sensitivity_portion, preferred_element_type=jnp.float32)
        slope_term = jax.nn.sigmoid(linear) * size_part[None, :]
        upstream = lax.dynamic_slice_in_dim(block_adjoint, group_index * per_group, per_group, 0)
        value_adjoint = (
            (upstream.T[:, :, None] * slope_term.reshape(row_count, per_group, block_width))
            .reshape(row_count, cluster_extent)
            .astype(jnp.bfloat16)
        )
        product = lax.dot_general(
            value_adjoint,
            sensitivity_portion,
            (((1,), (1,)), ((), ())),
            preferred_element_type=jnp.float32,
        )
        return running + product

    direct = lax.fori_loop(
        0, cluster_ordinal, pull_group, jnp.zeros((row_count, factor_count), jnp.float32)
    )
    direct = direct.reshape(date_count, path_count, factor_count)
    summed = lax.psum(direct, "trade")
    shock_gradient = reverse_chain(summed, persistence_ratio)
    return (exposure_profile, shock_gradient)


def solution(mesh):
    return jax.shard_map(
        shards,
        mesh=mesh,
        in_specs=(
            P(("grp", "date"), "path", None),
            P(("grp", "date"), None),
            P(None, ("grp", "trade")),
            P(("grp", "trade")),
            P(("grp", "trade")),
            P(("grp", "trade")),
            P(("grp", "date"), "trade"),
        ),
        out_specs=(P(("grp", "date"), "trade"), P(("grp", "date"), "path", None)),
        check_vma=False,
    )
```

profile of v0, /device:TPU:0, one launch (start us, length us, event | category | flops | bytes accessed | tf_op | source)
XLA Modules:
  0.0 200.2 jit_solution(7079904627721618631)
XLA Ops:
  8.8 5.1 %all-gather = f32[2,1,128]{2,1,0:T(1,128)S(1)} all-gather(f32[1,1,128]{2,1,0:T(1,128)S(1)} %get-tuple-element.550), channel_id=1, replica_groups=mesh['grp'=2,'trade'=4,'date'=2,'path'=2] {'date'}, dimensions={0}, use_global_device_ids=true | all-gather | bytes 1536 | tf_op jit(solution)/shard_map/all_gather | solution.py:13
  14.8 4.9 %all_gather.20 = f32[2,128,128]{2,1,0:T(8,128)S(1)} all-gather(f32[1,128,128]{2,1,0:T(8,128)S(1)} %multiply_add_fusion), channel_id=1, replica_groups=mesh['grp'=2,'trade'=4,'date'=2,'path'=2] {'date'}, dimensions={0}, use_global_device_ids=true | all-gather | bytes 196608 | tf_op jit(solution)/shard_map/all_gather | solution.py:13
  20.9 41.0 %while.57 = (s32[]{:T(128)}, f32[64,512]{1,0:T(8,128)S(1)}, bf16[128,8192]{1,0:T(8,128)(2,1)}, bf16[512,128]{1,0:T(8,128)(2,1)S(1)}, f32[8192]{0:T(1024)}, /*ind...) while((s32[]{:T(128)}, f32[64,512]{1,0:T(8,128)S(1)}, ...), condition=%wide.region_4.5_spmd, body=%wide.region_2.4_spmd.sunk | while | flops 69203976 | bytes 293085 | solution.py:91
  21.7 1.8 bitcast_reduce_fusion.2
  24.2 1.8 bitcast_reduce_fusion.2
  26.8 1.8 bitcast_reduce_fusion.2
  29.4 1.8 bitcast_reduce_fusion.2
  31.9 1.8 bitcast_reduce_fusion.2
  34.5 1.8 bitcast_reduce_fusion.2
  37.0 1.8 bitcast_reduce_fusion.2
  42.2 1.8 bitcast_reduce_fusion.2
  44.7 1.8 bitcast_reduce_fusion.2
  47.3 1.8 bitcast_reduce_fusion.2
  52.4 1.8 bitcast_reduce_fusion.2
  55.0 1.8 bitcast_reduce_fusion.2
  57.5 1.8 bitcast_reduce_fusion.2
  60.1 1.8 bitcast_reduce_fusion.2
  63.1 21.4 %reduce-scatter.2.cloned.1.call-done = f32[32,512]{1,0:T(8,128)} async-done(((f32[128,512]{1,0:T(8,128)}), f32[32,512]{1,0:T(8,128)}) %reduce-scatter.2.cloned.1.call-update) | async-done | bytes 65552 | tf_op jit(solution)/shard_map/reduce_scatter | solution.py:102
  85.6 13.8 %all_gather.21 = f32[128,512]{1,0:T(8,128)S(1)} all-gather(f32[32,512]{1,0:T(8,128)S(1)} %get-tuple-element.544), channel_id=1, replica_groups=mesh['grp'=2,'trade'=4,'date'=2,'path'=2] {'trade'}, dimensions={0}, use_global_device_ids=true | all-gather | bytes 327680 | tf_op jit(solution)/shard_map/all_gather | solution.py:111
  99.7 50.3 %while.59 = (s32[]{:T(128)}, f32[512,128]{1,0:T(8,128)S(1)}, f32[64,512]{1,0:T(8,128)S(1)}, bf16[128,8192]{1,0:T(8,128)(2,1)}, bf16[512,128]{1,0:T(8,128)(2,1)S(...) while((s32[]{:T(128)}, f32[512,128]{1,0:T(8,128)S(1)}, ...), condition=%wide.region_9.10_spmd.clone, body=%wide.region_8.9_spmd.clone.sunk | while | flops 135921680 | bytes 3063530 | solution.py:136
  150.8 4.2 %all-gather.1 = f32[2,1,128]{2,1,0:T(1,128)S(1)} all-gather(f32[1,1,128]{2,1,0:T(1,128)S(1)} %get-tuple-element.546), channel_id=1, replica_groups=mesh['grp'=2,'trade'=4,'date'=2,'path'=2] {'date'}, dimensions={0}, use_global_device_ids=true | all-gather | bytes 1536 | tf_op jit(solution)/shard_map/all_gather | solution.py:13
  155.1 3.4 %psum.14 = f32[4,32]{0,1:T(8,128)S(1)} all-reduce(f32[4,32]{0,1:T(8,128)S(1)} %bitcast.153), channel_id=1, replica_groups=mesh['grp'=2,'trade'=4,'date'=2,'path'=2] {'path'}, use_global_device_ids=true, to_apply=%region_7.8 | all-reduce | flops 128 | bytes 1024 | tf_op jit(solution)/shard_map/psum | solution.py:105
  159.1 25.7 %all-reduce.2.cloned.1.call-done = f32[4,128,128]{2,1,0:T(8,128)} async-done(((f32[4,128,128]{2,1,0:T(8,128)}), f32[4,128,128]{2,1,0:T(8,128)}) %all-reduce.2.cloned.1.call-update) | async-done | bytes 262160 | tf_op jit(solution)/shard_map/psum | solution.py:140
  185.8 4.9 %all_gather.23 = f32[2,128,128]{2,1,0:T(8,128)S(1)} all-gather(f32[1,128,128]{2,1,0:T(8,128)S(1)} %add_multiply_fusion), channel_id=1, replica_groups=mesh['grp'=2,'trade'=4,'date'=2,'path'=2] {'date'}, dimensions={0}, use_global_device_ids=true | all-gather | bytes 196608 | tf_op jit(solution)/shard_map/all_gather | solution.py:13
  (161 shorter events, 76.8 us)
Async XLA Ops:
  7.2 13.6 %copy-start = (f32[4,128,128]{2,1,0:T(8,128)S(1)}, f32[4,128,128]{2,1,0:T(8,128)}, u32[]{:S(2)}) copy-start(f32[4,128,128]{2,1,0:T(8,128)} %param.15) | copy-start | bytes 786436
  7.2 77.3 %reduce-scatter.2.cloned.1.call-start = ((), (), s32[]{:S(2)}) async-start(), calls=%async_computation.1 | async-start | bytes 327680 | tf_op jit(solution)/shard_map/reduce_scatter | solution.py:102
  20.8 41.0 %copy-start.2 = (s32[64]{0:T(128)S(1)}, s32[64]{0:T(128)}, u32[]{:S(2)}) copy-start(s32[64]{0:T(128)} %param.19) | copy-start | bytes 772
  20.9 42.2 %copy-start.3 = (f32[4,32]{1,0:T(4,128)S(1)}, f32[4,32]{1,0:T(4,128)}, u32[]{:S(2)}) copy-start(f32[4,32]{1,0:T(4,128)} %param.21) | copy-start | bytes 1540
  20.9 63.7 %copy-start.4 = (f32[32]{0:T(128)S(1)}, f32[32]{0:T(128)}, u32[]{:S(2)}) copy-start(f32[32]{0:T(128)} %param.20) | copy-start | bytes 388
  63.0 121.9 %all-reduce.2.cloned.1.call-start = ((), (), s32[]{:S(2)}) async-start(), calls=%async_computation.2 | async-start | bytes 524288 | tf_op jit(solution)/shard_map/psum | solution.py:140
  150.0 0.7 copy-start.1
Sparse Core Ops, SparseCore 0:
  63.1 21.3 reduce-scatter.1
  150.9 33.9 all-reduce.1
where the time goes:
time: 202 us; the launch traced here: 200 us
  matrix products  54.4 us (27%)
  waiting for transfers between devices  47.1 us (23%)
  local copies, waits for them, and re-layouts  38.5 us (19%)
  blocking collectives  36.4 us (18%)
  between operations  14.2 us (7%)
  other arithmetic  8.08 us (4%)
    dot_general x16, matrix products, value_group(): jnp.dot(state_bf, sensitivity_portion, preferred_element_type=jnp.float32)  28 us
    psum x1, waiting for transfers between devices, shards(): summed = lax.psum(direct, 'trade')  25.7 us
    dot_general x16, matrix products, pull_group(): lax.dot_general(value_adjoint, sensitivity_portion, (((1,), (1,)), ((), (...  25.1 us
    reduce_scatter x1, waiting for transfers between devices, shards(): lax.psum_scatter(partial_value, 'trade', scatter_dimension=0, tiled=True)  21.4 us
    all_gather x4, blocking collectives, entering(): everything = jax.tree.map(lambda part: lax.all_gather(part, axis), value)  19.2 us
    all_gather x1, blocking collectives, shards(): gathered = lax.all_gather(net_adjoint, 'trade', axis=0, tiled=True)  13.8 us
    dynamic_slice x16, local copies, waits for them, and re-layouts, value_group(): lax.dynamic_slice_in_dim(signed_notional, opening_offset, cluster_extent, 0)  12.2 us
    dynamic_slice x16, local copies, waits for them, and re-layouts, pull_group(): lax.dynamic_slice_in_dim(signed_notional, opening_offset, cluster_extent, 0)  12.2 us
  transfers between devices with their start and end apart: 2, of which 2 were waited for; matrix products, arithmetic and copies ran while one was open for 0% of the time, Pallas kernels for 0%

commit v1 on v0

--- a/solution.py
+++ b/solution.py
@@ -137,7 +137,7 @@
         0, cluster_ordinal, pull_group, jnp.zeros((row_count, factor_count), jnp.float32)
     )
     direct = direct.reshape(date_count, path_count, factor_count)
-    summed = lax.psum(direct, "trade")
+    summed = jnp.sum(lax.all_gather(direct, "trade"), axis=0)
     shock_gradient = reverse_chain(summed, persistence_ratio)
     return (exposure_profile, shock_gradient)
 

time: 202 us -> 193 us (0.955)
  waiting for transfers between devices: 47.1 us -> 39.7 us
    psum x1 -> x0, waiting for transfers between devices: 25.7 us -> none  [shards(): summed = lax.psum(direct, 'trade')]
    all_gather x0 -> x1, waiting for transfers between devices: none -> 18.3 us  [shards(): summed = jnp.sum(lax.all_gather(direct, 'trade'), axis=0)]
where the time goes in v1:
time: 193 us; the launch traced here: 191 us
  matrix products  54.4 us (28%)
  waiting for transfers between devices  39.7 us (21%)
  local copies, waits for them, and re-layouts  38.5 us (20%)
  blocking collectives  36.4 us (19%)
  between operations  14.2 us (7%)
  other arithmetic  6.68 us (3%)
    dot_general x16, matrix products, value_group(): jnp.dot(state_bf, sensitivity_portion, preferred_element_type=jnp.float32)  28 us
    dot_general x16, matrix products, pull_group(): lax.dot_general(value_adjoint, sensitivity_portion, (((1,), (1,)), ((), (...  25.1 us
    reduce_scatter x1, waiting for transfers between devices, shards(): lax.psum_scatter(partial_value, 'trade', scatter_dimension=0, tiled=True)  21.4 us
    all_gather x4, blocking collectives, entering(): everything = jax.tree.map(lambda part: lax.all_gather(part, axis), value)  19.2 us
    all_gather x1, waiting for transfers between devices, shards(): summed = jnp.sum(lax.all_gather(direct, 'trade'), axis=0)  18.3 us
    all_gather x1, blocking collectives, shards(): gathered = lax.all_gather(net_adjoint, 'trade', axis=0, tiled=True)  13.8 us
    dynamic_slice x16, local copies, waits for them, and re-layouts, value_group(): lax.dynamic_slice_in_dim(signed_notional, opening_offset, cluster_extent, 0)  12.2 us
    dynamic_slice x16, local copies, waits for them, and re-layouts, pull_group(): lax.dynamic_slice_in_dim(signed_notional, opening_offset, cluster_extent, 0)  12.2 us
  transfers between devices with their start and end apart: 2, of which 2 were waited for; matrix products, arithmetic and copies ran while one was open for 0% of the time, Pallas kernels for 0%

profile of v1, /device:TPU:0, one launch (start us, length us, event | category | flops | bytes accessed | tf_op | source)
XLA Modules:
  0.0 191.5 jit_solution(786265495929406652)
XLA Ops:
  8.8 5.1 %all-gather = f32[2,1,128]{2,1,0:T(1,128)S(1)} all-gather(f32[1,1,128]{2,1,0:T(1,128)S(1)} %get-tuple-element.550), channel_id=1, replica_groups=mesh['grp'=2,'trade'=4,'date'=2,'path'=2] {'date'}, dimensions={0}, use_global_device_ids=true | all-gather | bytes 1536 | tf_op jit(solution)/shard_map/all_gather | solution.py:13
  14.8 4.9 %all_gather.23 = f32[2,128,128]{2,1,0:T(8,128)S(1)} all-gather(f32[1,128,128]{2,1,0:T(8,128)S(1)} %multiply_add_fusion), channel_id=1, replica_groups=mesh['grp'=2,'trade'=4,'date'=2,'path'=2] {'date'}, dimensions={0}, use_global_device_ids=true | all-gather | bytes 196608 | tf_op jit(solution)/shard_map/all_gather | solution.py:13
  20.9 41.0 %while.57 = (s32[]{:T(128)}, f32[64,512]{1,0:T(8,128)S(1)}, bf16[128,8192]{1,0:T(8,128)(2,1)}, bf16[512,128]{1,0:T(8,128)(2,1)S(1)}, f32[8192]{0:T(1024)}, /*ind...) while((s32[]{:T(128)}, f32[64,512]{1,0:T(8,128)S(1)}, ...), condition=%wide.region_4.5_spmd, body=%wide.region_2.4_spmd.sunk | while | flops 69203976 | bytes 293085 | solution.py:91
  21.7 1.8 bitcast_reduce_fusion.2
  24.2 1.8 bitcast_reduce_fusion.2
  26.8 1.8 bitcast_reduce_fusion.2
  29.4 1.8 bitcast_reduce_fusion.2
  31.9 1.8 bitcast_reduce_fusion.2
  34.5 1.8 bitcast_reduce_fusion.2
  37.0 1.8 bitcast_reduce_fusion.2
  42.2 1.8 bitcast_reduce_fusion.2
  44.7 1.8 bitcast_reduce_fusion.2
  47.3 1.8 bitcast_reduce_fusion.2
  52.4 1.8 bitcast_reduce_fusion.2
  55.0 1.8 bitcast_reduce_fusion.2
  57.5 1.8 bitcast_reduce_fusion.2
  60.1 1.8 bitcast_reduce_fusion.2
  63.1 21.4 %reduce-scatter.2.cloned.1.call-done = f32[32,512]{1,0:T(8,128)} async-done(((f32[128,512]{1,0:T(8,128)}), f32[32,512]{1,0:T(8,128)}) %reduce-scatter.2.cloned.1.call-update) | async-done | bytes 65552 | tf_op jit(solution)/shard_map/reduce_scatter | solution.py:102
  85.6 13.8 %all_gather.24 = f32[128,512]{1,0:T(8,128)S(1)} all-gather(f32[32,512]{1,0:T(8,128)S(1)} %get-tuple-element.544), channel_id=1, replica_groups=mesh['grp'=2,'trade'=4,'date'=2,'path'=2] {'trade'}, dimensions={0}, use_global_device_ids=true | all-gather | bytes 327680 | tf_op jit(solution)/shard_map/all_gather | solution.py:111
  99.7 50.3 %while.59 = (s32[]{:T(128)}, f32[512,128]{1,0:T(8,128)S(1)}, f32[64,512]{1,0:T(8,128)S(1)}, bf16[128,8192]{1,0:T(8,128)(2,1)}, bf16[512,128]{1,0:T(8,128)(2,1)S(...) while((s32[]{:T(128)}, f32[512,128]{1,0:T(8,128)S(1)}, ...), condition=%wide.region_9.10_spmd.clone, body=%wide.region_8.9_spmd.clone.sunk | while | flops 135921680 | bytes 3063530 | solution.py:136
  150.8 4.2 %all-gather.1 = f32[2,1,128]{2,1,0:T(1,128)S(1)} all-gather(f32[1,1,128]{2,1,0:T(1,128)S(1)} %get-tuple-element.546), channel_id=1, replica_groups=mesh['grp'=2,'trade'=4,'date'=2,'path'=2] {'date'}, dimensions={0}, use_global_device_ids=true | all-gather | bytes 1536 | tf_op jit(solution)/shard_map/all_gather | solution.py:13
  155.1 3.4 %psum.7 = f32[4,32]{0,1:T(8,128)S(1)} all-reduce(f32[4,32]{0,1:T(8,128)S(1)} %bitcast.153), channel_id=1, replica_groups=mesh['grp'=2,'trade'=4,'date'=2,'path'=2] {'path'}, use_global_device_ids=true, to_apply=%region_7.8 | all-reduce | flops 128 | bytes 1024 | tf_op jit(solution)/shard_map/psum | solution.py:105
  159.1 18.3 %all-gather.4.cloned.1.call-done = f32[4,4,128,128]{3,2,1,0:T(8,128)} async-done(((f32[1,4,128,128]{3,2,1,0:T(8,128)}), f32[4,4,128,128]{3,2,1,0:T(8,128)}) %all-gather.4.cloned.1.call-update) | async-done | bytes 1048592 | tf_op jit(solution)/shard_map/all_gather | solution.py:140
  178.8 4.9 %all_gather.27 = f32[2,128,128]{2,1,0:T(8,128)S(1)} all-gather(f32[1,128,128]{2,1,0:T(8,128)S(1)} %add_multiply_fusion), channel_id=1, replica_groups=mesh['grp'=2,'trade'=4,'date'=2,'path'=2] {'date'}, dimensions={0}, use_global_device_ids=true | all-gather | bytes 196608 | tf_op jit(solution)/shard_map/all_gather | solution.py:13
  (162 shorter events, 75.4 us)
Async XLA Ops:
  7.2 13.6 %copy-start = (f32[4,128,128]{2,1,0:T(8,128)S(1)}, f32[4,128,128]{2,1,0:T(8,128)}, u32[]{:S(2)}) copy-start(f32[4,128,128]{2,1,0:T(8,128)} %param.15) | copy-start | bytes 786436
  7.2 77.3 %reduce-scatter.2.cloned.1.call-start = ((), (), s32[]{:S(2)}) async-start(), calls=%async_computation.1 | async-start | bytes 327680 | tf_op jit(solution)/shard_map/reduce_scatter | solution.py:102
  20.8 41.0 %copy-start.2 = (s32[64]{0:T(128)S(1)}, s32[64]{0:T(128)}, u32[]{:S(2)}) copy-start(s32[64]{0:T(128)} %param.19) | copy-start | bytes 772
  20.9 42.2 %copy-start.3 = (f32[4,32]{1,0:T(4,128)S(1)}, f32[4,32]{1,0:T(4,128)}, u32[]{:S(2)}) copy-start(f32[4,32]{1,0:T(4,128)} %param.21) | copy-start | bytes 1540
  20.9 63.7 %copy-start.4 = (f32[32]{0:T(128)S(1)}, f32[32]{0:T(128)}, u32[]{:S(2)}) copy-start(f32[32]{0:T(128)} %param.20) | copy-start | bytes 388
  63.0 114.5 %all-gather.4.cloned.1.call-start = ((), (), s32[]{:S(2)}) async-start(), calls=%async_computation.2 | async-start | bytes 1310720 | tf_op jit(solution)/shard_map/all_gather | solution.py:140
  150.0 0.7 copy-start.1
Sparse Core Ops, SparseCore 0:
  63.1 21.3 reduce-scatter.1
  150.9 26.5 all-gather.3
